TPU v7x, 128 devices: a whole 4x4x4 slice. The times are simulated.
128 devices in a mesh: sec: 4 (over x), op: 32 (over z, y, core).
Axes of the slice: x: 4, y: 4, z: 4, core: 2. Of those that a mesh axis runs over, the one named last changes fastest.
Arguments:
- wavefunction: bfloat16 [4, 1024, 1024], P('sec'), may hold values from -6 to 6
- left_operator: bfloat16 [128, 4, 1024, 1024], P('op', 'sec'), may hold values from -0.011048543 to 0.35355339
- right_operator: bfloat16 [128, 1024, 1024], P('op'), may hold values from -0.125 to 1.125
- sector_size: int32 [4], replicated, may hold values from 512 to 1024
- term_shift: int32 [128], replicated, may hold values from 0 to 3, as said below
Outputs:
- sigma: float32 [4, 1024, 1024], P('sec', 'op')
- residual: float32 [4, 1024, 1024], P('sec', 'op')
Inputs may be any that keep to these rules, and one draw needn't show every extreme that they name: `term_shift`: among the 4 terms of one index of op (terms g * 4 to g * 4 + 3), the shifts are distinct.
All inputs are finite; a program needn't handle non-finite values.
Results may differ from a plain program's by a relative error of at most 0.0025.
Values may be sent and summed in bfloat16 or wider, within the bound.
A program may use at most 128 MiB of HBM per device.

v0:
```python
import jax
import jax.numpy as jnp
from jax import lax
from jax.sharding import Mesh
from jax.sharding import PartitionSpec as P

OP = ("op_0", "op_1", "op_2")
SEC_OP = ("sec", "op_0", "op_1", "op_2")


def over_axes(x, axes):
    for axis in axes:
        x = lax.psum(x, axis)
    return x


def per_device(wavefunction, left_operator, right_operator, sector_size, term_shift):
    sec_count = lax.axis_size("sec")
    op_count = lax.axis_size(OP)
    sec_index = lax.axis_index("sec")
    op_index = lax.axis_index(OP)
    term_count = left_operator.shape[0]
    sector_rows = wavefunction.shape[1]
    col_count = wavefunction.shape[2]
    row_count = sector_rows // op_count
    positions = jnp.arange(sector_rows, dtype=jnp.int32)
    own_size = sector_size[sec_index]
    masked = wavefunction[0] * (positions < own_size).astype(jnp.bfloat16)[:, None]
    left_image = jnp.einsum(
        "tmn,nk->tmk", left_operator[:, 0], masked, preferred_element_type=jnp.float32
    ).astype(jnp.bfloat16)
    right_image = jnp.einsum(
        "tmk,tkl->tml", left_image, right_operator, preferred_element_type=jnp.float32
    ).astype(jnp.bfloat16)
    local_shifts = lax.dynamic_slice_in_dim(term_shift, op_index * term_count, term_count)
    targets = (sec_index + local_shifts) % sec_count
    routing_onehot = (targets[:, None] == jnp.arange(sec_count, dtype=jnp.int32)[None, :]).astype(
        jnp.bfloat16
    )
    outgoing = jnp.einsum(
        "tn,tmk->nmk", routing_onehot, right_image, preferred_element_type=jnp.float32
    ).astype(jnp.bfloat16)
    blocks = outgoing.reshape(sec_count * op_count, row_count, col_count)
    incoming = lax.all_to_all(blocks, SEC_OP, split_axis=0, concat_axis=0, tiled=True)
    summed = jnp.sum(incoming, axis=0, dtype=jnp.float32)
    global_rows = op_index * row_count + jnp.arange(row_count, dtype=jnp.int32)
    out_mask = (global_rows < own_size).astype(jnp.float32)
    sigma_rows = summed * out_mask[:, None]
    state_rows = lax.dynamic_slice_in_dim(masked, op_index * row_count, row_count, 0).astype(
        jnp.float32
    )
    norm_sum, cross_sum = (
        over_axes(jnp.sum(state_rows * state_rows), SEC_OP),
        over_axes(jnp.sum(state_rows * sigma_rows), SEC_OP),
    )
    energy = cross_sum / norm_sum
    residual_rows = sigma_rows - energy * state_rows
    return (sigma_rows[None], residual_rows[None])


def solution(mesh):
    finer = Mesh(mesh.devices.reshape(mesh.shape["sec"], 4, 4, 2), ("sec", "op_0", "op_1", "op_2"))
    return jax.shard_map(
        per_device,
        mesh=finer,
        in_specs=(P("sec", None, None), P(OP, "sec", None, None), P(OP, None, None), P(), P()),
        out_specs=(P("sec", OP, None), P("sec", OP, None)),
        check_vma=False,
    )
```

profile of v0, /device:TPU:1, one launch (start us, length us, event | category | flops | bytes accessed | tf_op | source)
XLA Modules:
  0.0 231.8 jit_solution(6037880737334125754)
XLA Ops:
  0.6 1.2 dynamic_slice.10
  1.9 0.6 fusion.16
  2.5 12.7 %fusion.5 = bf16[1024,4,1024]{2,0,1:T(8,128)(2,1)S(1)} fusion(bf16[4,1,1024,1024]{3,2,1,0:T(8,128)(2,1)} %param.6, bf16[1,1024,1024]{2,1,0:T(8,128)(2,1)} %param.5, bf16[1024]{0:T(1024)(128)(2,1)S(1)} %fusion.16), kind=kOutput, calls=%fused_computation.8 | convolution fusion | flops 8598323200 | bytes 18876416 | tf_op jit(solution)/shard_map/tmn,nk->tmk/dot_general | solution.py:29
  15.2 0.0 copy-start
  15.2 22.8 %copy.19 = bf16[1024,4,1024]{2,1,0:T(4,128)(2,1)} copy(bf16[1024,4,1024]{2,0,1:T(8,128)(2,1)S(1)} %fusion.5) | data formatting | bytes 16777216
  38.0 0.0 copy-done
  38.0 0.1 and_select_fusion
  38.1 14.9 %fusion.3 = bf16[4,1024,1024]{2,1,0:T(8,128)(2,1)S(1)} fusion(bf16[4,1024,1024]{2,1,0:T(8,128)(2,1)} %param.7, bf16[4,1024,1024]{1,0,2:T(4,128)(2,1)} %bitcast.24), kind=kOutput, calls=%fused_computation.6 | convolution fusion | flops 8589934592 | bytes 25165824 | tf_op jit(solution)/shard_map/tmk,tkl->tml/dot_general | solution.py:32
  53.0 7.5 %fusion.8 = bf16[4,1024,1024]{2,0,1:T(4,128)(2,1)} fusion(bf16[4,1024,1024]{2,1,0:T(8,128)(2,1)S(1)} %fusion.3, s32[4]{0:T(128)S(1)} %and_select_fusion), kind=kOutput, calls=%fused_computation.9 | convolution fusion | flops 37748752 | bytes 16777232 | tf_op jit(solution)/shard_map/tn,tmk->nmk/dot_general | solution.py:40
  60.4 9.5 %copy.7 = bf16[4,1024,1024]{2,1,0:T(8,128)(2,1)} copy(bf16[4,1024,1024]{2,0,1:T(4,128)(2,1)} %fusion.8) | data formatting | bytes 16777216 | tf_op jit(solution)/shard_map/convert_element_type | solution.py:42
  69.9 12.0 %all-to-all-start = ((bf16[128,32,1024]{2,1,0:T(8,128)(2,1)}), bf16[128,32,1024]{2,1,0:T(8,128)(2,1)}, u32[]{:S(2)}, u32[]{:S(2)}) async-start(bf16[128,32,1024]{2,1,0:T(8,128)(2,1)} %bitcast.23), calls=%async_computation | async-start | bytes 16777216 | tf_op jit(solution)/shard_map/all_to_all | solution.py:44
  81.9 0.1 dynamic-slice
  81.9 0.6 compare_convert_fusion
  82.6 105.4 %all-to-all-done = bf16[128,32,1024]{2,1,0:T(8,128)(2,1)} async-done(((bf16[128,32,1024]{2,1,0:T(8,128)(2,1)}), bf16[128,32,1024]{2,1,0:T(8,128)(2,1)}, u32[]{:S(2)}, u32[]{:S(2)}) %all-to-all-start) | async-done | bytes 8388640 | tf_op jit(solution)/shard_map/all_to_all | solution.py:44
  188.0 5.2 %convert_reduce_fusion = f32[32,1024]{1,0:T(8,128)S(1)} fusion(bf16[128,32,1024]{2,1,0:T(8,128)(2,1)} %all-to-all-done), kind=kLoop, calls=%fused_computation.1 | loop fusion | flops 8355840 | bytes 8519680 | tf_op jit(solution)/shard_map/reduce_sum | solution.py:45
  193.2 0.7 bitcast_multiply_fusion
  194.0 1.6 fusion.13
  195.5 6.7 %all-reduce.2 = (f32[]{:T(128)}, f32[]{:T(128)}) all-reduce(f32[]{:T(128)} %get-tuple-element.3, f32[]{:T(128)} %get-tuple-element.2), channel_id=1, replica_groups=mesh['sec'=4,'op_0'=4,'op_1'=4,'op_2'=2] {'sec'}, use_global_device_ids=true, to_apply=%region_2.3 | all-reduce | flops 2 | bytes 16 | tf_op jit(solution)/shard_map/psum | solution.py:13
  202.2 7.9 %all-reduce.1 = (f32[]{:T(128)}, f32[]{:T(128)}) all-reduce(f32[]{:T(128)} %get-tuple-element.8, f32[]{:T(128)} %get-tuple-element.9), channel_id=1, replica_groups=mesh['sec'=4,'op_0'=4,'op_1'=4,'op_2'=2] {'op_0'}, use_global_device_ids=true, to_apply=%region_3.4 | all-reduce | flops 2 | bytes 16 | tf_op jit(solution)/shard_map/psum | solution.py:13
  210.1 9.3 %all-reduce = (f32[]{:T(128)}, f32[]{:T(128)}) all-reduce(f32[]{:T(128)} %get-tuple-element.6, f32[]{:T(128)} %get-tuple-element.7), channel_id=1, replica_groups=mesh['sec'=4,'op_0'=4,'op_1'=4,'op_2'=2] {'op_1'}, use_global_device_ids=true, to_apply=%region_4.5 | all-reduce | flops 2 | bytes 16 | tf_op jit(solution)/shard_map/psum | solution.py:13
  219.4 9.5 %all-reduce.3 = (f32[]{:T(128)}, f32[]{:T(128)}) all-reduce(f32[]{:T(128)} %get-tuple-element.4, f32[]{:T(128)} %get-tuple-element.5), channel_id=1, replica_groups=mesh['sec'=4,'op_0'=4,'op_1'=4,'op_2'=2] {'op_2'}, use_global_device_ids=true, to_apply=%region_5.6 | all-reduce | flops 2 | bytes 16 | tf_op jit(solution)/shard_map/psum | solution.py:13
  230.2 1.6 fusion.15
Async XLA Ops:
  15.2 22.8 %copy-start = (s32[128]{0:T(128)S(1)}, s32[128]{0:T(128)}, u32[]{:S(2)}) copy-start(s32[128]{0:T(128)} %param.9) | copy-start | bytes 1540
  69.9 118.1 %all-to-all-start = ((bf16[128,32,1024]{2,1,0:T(8,128)(2,1)}), bf16[128,32,1024]{2,1,0:T(8,128)(2,1)}, u32[]{:S(2)}, u32[]{:S(2)}) async-start(bf16[128,32,1024]{2,1,0:T(8,128)(2,1)} %bitcast.23), calls=%async_computation | async-start | bytes 16777216 | tf_op jit(solution)/shard_map/all_to_all | solution.py:44
where the time goes:
time: 232 us
  waiting for transfers between devices  105 us (45%)
  matrix products  35 us (15%)
  local copies, waits for them, and re-layouts  33.5 us (14%)
  blocking collectives  33.4 us (14%)
  starting transfers between devices  12 us (5%)
  other arithmetic  10.5 us (5%)
    all_to_all x1, waiting for transfers between devices, per_device(): lax.all_to_all(blocks, SEC_OP, split_axis=0, concat_axis=0, tiled=True)  105 us
    psum x4, blocking collectives, over_axes(): x = lax.psum(x, axis)  33.4 us
    unnamed x3, local copies, waits for them, and re-layouts  22.8 us
    dot_general x1, matrix products, per_device(): jnp.einsum('tmk,tkl->tml', left_image, right_operator, preferred_element_...  14.9 us
    dot_general x1, matrix products, per_device(): jnp.einsum('tmn,nk->tmk', left_operator[:, 0], masked, preferred_element_...  12.7 us
    all_to_all x1, starting transfers between devices, per_device(): lax.all_to_all(blocks, SEC_OP, split_axis=0, concat_axis=0, tiled=True)  12 us
    convert_element_type x1, local copies, waits for them, and re-layouts, per_device(): outgoing = jnp.einsum('tn,tmk->nmk', routing_onehot, right_image, preferr...  9.46 us
    dot_general x1, matrix products, per_device(): jnp.einsum('tn,tmk->nmk', routing_onehot, right_image, preferred_element_...  7.45 us
  transfers between devices with their start and end apart: 1, of which 1 were waited for; matrix products, arithmetic and copies ran while one was open for 0% of the time, Pallas kernels for 0%

commit v1 on v0

--- a/solution.py
+++ b/solution.py
@@ -10,7 +10,8 @@
 
 def over_axes(x, axes):
     for axis in axes:
-        x = lax.psum(x, axis)
+        y2 = jax.lax.all_gather(x, axis)
+        x = jnp.sum(y2, 0)
     return x
 
 

time: 232 us -> 248 us (1.069)
  local copies, waits for them, and re-layouts: 33.5 us -> 47.1 us
  other arithmetic: 10.5 us -> 15.6 us
  blocking collectives: 33.4 us -> 30.7 us
    psum x4 -> x0, blocking collectives: 33.4 us -> none  [over_axes(): x = lax.psum(x, axis)]
    unnamed x0 -> x4, blocking collectives: none -> 30.7 us
    unnamed x3 -> x31, local copies, waits for them, and re-layouts: 22.8 us -> 36.3 us
    reduce_sum x0 -> x8, other arithmetic: none -> 5.13 us  [over_axes(): x = jnp.sum(y2, 0)]
  transfers between devices with their start and end apart: 1 -> 1, of which waited for: 1 -> 1; matrix products, arithmetic and copies ran while one was open for 0% -> 1% of each run, Pallas kernels for 0% -> 0%
where the time goes in v1:
time: 248 us; the launch traced here: 247 us
  waiting for transfers between devices  105 us (42%)
  local copies, waits for them, and re-layouts  47.1 us (19%)
  matrix products  35 us (14%)
  blocking collectives  30.7 us (12%)
  other arithmetic  15.6 us (6%)
  starting transfers between devices  12 us (5%)
    all_to_all x1, waiting for transfers between devices, per_device(): lax.all_to_all(blocks, SEC_OP, split_axis=0, concat_axis=0, tiled=True)  105 us
    unnamed x31, local copies, waits for them, and re-layouts  36.3 us
    unnamed x4, blocking collectives  30.7 us
    dot_general x1, matrix products, per_device(): jnp.einsum('tmk,tkl->tml', left_image, right_operator, preferred_element_...  14.9 us
    dot_general x1, matrix products, per_device(): jnp.einsum('tmn,nk->tmk', left_operator[:, 0], masked, preferred_element_...  12.7 us
    all_to_all x1, starting transfers between devices, per_device(): lax.all_to_all(blocks, SEC_OP, split_axis=0, concat_axis=0, tiled=True)  12 us
    convert_element_type x1, local copies, waits for them, and re-layouts, per_device(): outgoing = jnp.einsum('tn,tmk->nmk', routing_onehot, right_image, preferr...  9.46 us
    dot_general x1, matrix products, per_device(): jnp.einsum('tn,tmk->nmk', routing_onehot, right_image, preferred_element_...  7.45 us
  transfers between devices with their start and end apart: 1, of which 1 were waited for; matrix products, arithmetic and copies ran while one was open for 1% of the time, Pallas kernels for 0%

profile of v1, /device:TPU:1, one launch (start us, length us, event | category | flops | bytes accessed | tf_op | source)
XLA Modules:
  0.0 247.3 jit_solution(12263125900290284244)
XLA Ops:
  0.6 1.2 dynamic_slice.10
  1.9 0.6 fusion.16
  2.5 12.7 %fusion.5 = bf16[1024,4,1024]{2,0,1:T(8,128)(2,1)S(1)} fusion(bf16[4,1,1024,1024]{3,2,1,0:T(8,128)(2,1)} %param.6, bf16[1,1024,1024]{2,1,0:T(8,128)(2,1)} %param.5, bf16[1024]{0:T(1024)(128)(2,1)S(1)} %fusion.16), kind=kOutput, calls=%fused_computation.8 | convolution fusion | flops 8598323200 | bytes 18876416 | tf_op jit(solution)/shard_map/tmn,nk->tmk/dot_general | solution.py:30
  15.2 0.0 copy-start
  15.2 22.8 %copy.19 = bf16[1024,4,1024]{2,1,0:T(4,128)(2,1)} copy(bf16[1024,4,1024]{2,0,1:T(8,128)(2,1)S(1)} %fusion.5) | data formatting | bytes 16777216
  38.0 0.0 copy-done
  38.0 0.1 and_select_fusion
  38.1 14.9 %fusion.3 = bf16[4,1024,1024]{2,1,0:T(8,128)(2,1)S(1)} fusion(bf16[4,1024,1024]{2,1,0:T(8,128)(2,1)} %param.7, bf16[4,1024,1024]{1,0,2:T(4,128)(2,1)} %bitcast.36), kind=kOutput, calls=%fused_computation.6 | convolution fusion | flops 8589934592 | bytes 25165824 | tf_op jit(solution)/shard_map/tmk,tkl->tml/dot_general | solution.py:33
  53.0 7.5 %fusion.8 = bf16[4,1024,1024]{2,0,1:T(4,128)(2,1)} fusion(bf16[4,1024,1024]{2,1,0:T(8,128)(2,1)S(1)} %fusion.3, s32[4]{0:T(128)S(1)} %and_select_fusion), kind=kOutput, calls=%fused_computation.9 | convolution fusion | flops 37748752 | bytes 16777232 | tf_op jit(solution)/shard_map/tn,tmk->nmk/dot_general | solution.py:41
  60.4 9.5 %copy.7 = bf16[4,1024,1024]{2,1,0:T(8,128)(2,1)} copy(bf16[4,1024,1024]{2,0,1:T(4,128)(2,1)} %fusion.8) | data formatting | bytes 16777216 | tf_op jit(solution)/shard_map/convert_element_type | solution.py:43
  69.9 0.0 copy-start.4
  69.9 12.0 %all-to-all-start = ((bf16[128,32,1024]{2,1,0:T(8,128)(2,1)}), bf16[128,32,1024]{2,1,0:T(8,128)(2,1)}, u32[]{:S(2)}, u32[]{:S(2)}) async-start(bf16[128,32,1024]{2,1,0:T(8,128)(2,1)} %bitcast.35), calls=%async_computation | async-start | bytes 16777216 | tf_op jit(solution)/shard_map/all_to_all | solution.py:45
  81.9 0.0 copy-start.3
  81.9 0.0 copy-start.2
  81.9 0.0 copy-start.1
  81.9 0.1 dynamic-slice.8
  82.0 0.0 copy-done.4
  82.0 0.6 dynamic-slice
  82.6 0.6 compare_convert_fusion
  83.2 104.8 %all-to-all-done = bf16[128,32,1024]{2,1,0:T(8,128)(2,1)} async-done(((bf16[128,32,1024]{2,1,0:T(8,128)(2,1)}), bf16[128,32,1024]{2,1,0:T(8,128)(2,1)}, u32[]{:S(2)}, u32[]{:S(2)}) %all-to-all-start) | async-done | bytes 8388640 | tf_op jit(solution)/shard_map/all_to_all | solution.py:45
  188.0 5.2 %convert_reduce_fusion = f32[32,1024]{1,0:T(8,128)S(1)} fusion(bf16[128,32,1024]{2,1,0:T(8,128)(2,1)} %all-to-all-done), kind=kLoop, calls=%fused_computation.1 | loop fusion | flops 8355840 | bytes 8519680 | tf_op jit(solution)/shard_map/reduce_sum | solution.py:46
  193.2 1.6 fusion.13
  194.8 1.3 dynamic-update-slice
  196.1 1.3 dynamic-update-slice.4
  197.4 0.0 copy-done.3
  197.4 0.6 dynamic-slice.1
  198.0 6.0 %all-reduce.10 = (f32[4]{0:T(128)S(1)}, f32[4]{0:T(128)S(1)}) all-reduce(f32[4]{0:T(128)S(1)} %dynamic-update-slice, f32[4]{0:T(128)S(1)} %dynamic-update-slice.4), channel_id=1, replica_groups=mesh['sec'=4,'op_0'=4,'op_1'=4,'op_2'=2] {'sec'}, use_global_device_ids=true, to_apply=%add | all-reduce | flops 8 | bytes 64
  204.0 0.7 reduce_sum.109
  204.7 0.6 reduce_sum.104
  205.3 1.4 dynamic-update-slice.5
  206.7 1.4 dynamic-update-slice.1
  208.1 0.0 copy-done.2
  208.1 0.6 dynamic-slice.2
  208.7 7.3 %all-reduce.9 = (f32[4]{0:T(128)S(1)}, f32[4]{0:T(128)S(1)}) all-reduce(f32[4]{0:T(128)S(1)} %dynamic-update-slice.1, f32[4]{0:T(128)S(1)} %dynamic-update-slice.5), channel_id=1, replica_groups=mesh['sec'=4,'op_0'=4,'op_1'=4,'op_2'=2] {'op_0'}, use_global_device_ids=true, to_apply=%add.1 | all-reduce | flops 8 | bytes 64
  216.0 0.7 reduce_sum.110
  216.7 0.6 reduce_sum.105
  217.3 1.4 dynamic-update-slice.6
  218.7 1.4 dynamic-update-slice.2
  220.1 0.0 copy-done.1
  220.1 0.6 dynamic-slice.3
  220.7 8.6 %all-reduce.8 = (f32[4]{0:T(128)S(1)}, f32[4]{0:T(128)S(1)}) all-reduce(f32[4]{0:T(128)S(1)} %dynamic-update-slice.2, f32[4]{0:T(128)S(1)} %dynamic-update-slice.6), channel_id=1, replica_groups=mesh['sec'=4,'op_0'=4,'op_1'=4,'op_2'=2] {'op_1'}, use_global_device_ids=true, to_apply=%add.2 | all-reduce | flops 8 | bytes 64
  229.3 0.7 reduce_sum.111
  230.0 0.6 reduce_sum.106
  230.6 1.4 dynamic-update-slice.7
  232.0 1.4 dynamic-update-slice.3
  233.4 0.7 bitcast_multiply_fusion
  234.2 8.8 %all-reduce.11 = (f32[2]{0:T(128)S(1)}, f32[2]{0:T(128)S(1)}) all-reduce(f32[2]{0:T(128)S(1)} %dynamic-update-slice.3, f32[2]{0:T(128)S(1)} %dynamic-update-slice.7), channel_id=1, replica_groups=mesh['sec'=4,'op_0'=4,'op_1'=4,'op_2'=2] {'op_2'}, use_global_device_ids=true, to_apply=%add.3 | all-reduce | flops 4 | bytes 32
  243.0 0.6 reduce_sum.107
  243.6 0.7 reduce_sum.112
  245.7 1.6 fusion.15
  (8 shorter events, 0.0 us)
Async XLA Ops:
  15.2 22.8 %copy-start = (s32[128]{0:T(128)S(1)}, s32[128]{0:T(128)}, u32[]{:S(2)}) copy-start(s32[128]{0:T(128)} %param.9) | copy-start | bytes 1540
  69.9 12.1 %copy-start.4 = (u32[128]{0:T(128)S(1)}, u32[128]{0:T(128)}, u32[]{:S(2)}) copy-start(u32[128]{0:T(128)} %constant.48) | copy-start | bytes 1540
  69.9 118.1 %all-to-all-start = ((bf16[128,32,1024]{2,1,0:T(8,128)(2,1)}), bf16[128,32,1024]{2,1,0:T(8,128)(2,1)}, u32[]{:S(2)}, u32[]{:S(2)}) async-start(bf16[128,32,1024]{2,1,0:T(8,128)(2,1)} %bitcast.35), calls=%async_computation | async-start | bytes 16777216 | tf_op jit(solution)/shard_map/all_to_all | solution.py:45
  81.9 115.6 %copy-start.3 = (u32[128]{0:T(128)S(1)}, u32[128]{0:T(128)}, u32[]{:S(2)}) copy-start(u32[128]{0:T(128)} %constant.53) | copy-start | bytes 1540
  81.9 126.3 %copy-start.2 = (u32[128]{0:T(128)S(1)}, u32[128]{0:T(128)}, u32[]{:S(2)}) copy-start(u32[128]{0:T(128)} %constant.58) | copy-start | bytes 1540
  81.9 138.2 %copy-start.1 = (u32[128]{0:T(128)S(1)}, u32[128]{0:T(128)}, u32[]{:S(2)}) copy-start(u32[128]{0:T(128)} %constant.63) | copy-start | bytes 1540
